TPU v7x, 32 devices: a whole 2x2x4 slice. The times are simulated.
32 devices in a mesh: grp: 2 (over x), gx: 16 (over z, y, core).
Axes of the slice: x: 2, y: 2, z: 4, core: 2. Of those that a mesh axis runs over, the one named last changes fastest.
Arguments:
- voltages: bfloat16 [1024, 143360], P(('grp', 'gx')), parts along dimension 0, may hold values from -6 to 6
- taps: float32 [4, 4096], replicated, may hold values from -3 to 3
- weights: bfloat16 [2, 64, 256, 128], P(None, 'gx'), may hold values from -0.25 to 0.25
- antenna_weight_index: int32 [1024], P(('grp', 'gx')), parts along dimension 0, may hold values from 0 to 255
- flagged: int32 [1024], P(('grp', 'gx')), parts along dimension 0, may hold values 0 or 1
- trials: int32 [256], P(('grp', 'gx')), parts along dimension 0, may hold values from 0 to 63
Outputs:
- dedispersed: float32 [2, 32, 256, 64], P(None, None, ('grp', 'gx')), parts along dimension 2
There are 2 independent parts, one for each index of `grp`. A program takes and returns all parts, laid end to end along the dimension named above; an argument that names none is the same for every part. Nothing has to cross between parts.
All inputs are finite; a program needn't handle non-finite values. No bound on the sum of `flagged` on one device may be relied on, other than what follows from the above.
Results may differ from a plain program's by a relative error of at most 0.009.
Values may be sent and summed in bfloat16 or wider, within the bound.
A program may use at most 64 MiB of HBM per device.

v0:
```python
import math

import jax
import jax.numpy as jnp
from jax import lax
from jax.sharding import PartitionSpec as P

FRAME_COUNT = 32
FORWARD_LENGTH = 4096
TAP_COUNT = 4
CH_LO = 1024
WEIGHT_ROWS = 256


dm_unit = 0.173


def forward_table(nfft_len, first_bin, kept):
    bins = first_bin + jnp.arange(kept, dtype=jnp.int32)
    samples = jnp.arange(nfft_len, dtype=jnp.int32)
    modulo = bins[:, None] * samples[None, :] % nfft_len
    angles = modulo.astype(jnp.float32) * (2.0 * math.pi / nfft_len)
    return jnp.concatenate([jnp.cos(angles), -jnp.sin(angles)], 0).astype(jnp.bfloat16)


def inverse_table(length):
    chans = jnp.arange(length, dtype=jnp.int32)
    modulo = chans[:, None] * chans[None, :] % length
    angles = modulo.astype(jnp.float32) * (2.0 * math.pi / length)
    cosine = jnp.cos(angles)
    sine = jnp.sin(angles)
    return jnp.stack([jnp.stack([cosine, sine], 1), jnp.stack([-sine, cosine], 1)], 0).astype(
        jnp.bfloat16
    )


def chirp_apply(beams, trial_ids, channel_total):
    chans = jnp.arange(beams.shape[3], dtype=jnp.int32).astype(jnp.float32) / channel_total
    phase = (
        -2.0
        * math.pi
        * dm_unit
        * (trial_ids.astype(jnp.float32) + 1.0)[:, None]
        * (chans * chans)[None, :]
    )
    cosine = jnp.cos(phase)[None]
    sine = jnp.sin(phase)[None]
    real_part = beams[0].astype(jnp.float32)
    imag_part = beams[1].astype(jnp.float32)
    return jnp.stack(
        [real_part * cosine - imag_part * sine, real_part * sine + imag_part * cosine]
    ).astype(jnp.bfloat16)


def make_onehot(all_index):
    return (all_index[:, None] == jnp.arange(WEIGHT_ROWS, dtype=jnp.int32)[None, :]).astype(
        jnp.bfloat16
    )


def per_device(voltages, taps, weights, antenna_weight_index, flagged, trials):
    antenna_slice = voltages.shape[0]
    chan_local = weights.shape[1]
    channel_total = chan_local * lax.axis_size("gx")
    frame_samples = voltages.reshape(antenna_slice, FRAME_COUNT + TAP_COUNT - 1, FORWARD_LENGTH)
    running_sum = jnp.zeros((antenna_slice, FRAME_COUNT, FORWARD_LENGTH), jnp.float32)
    for tap_index in range(TAP_COUNT):
        running_sum = running_sum + taps[tap_index][None, None, :] * frame_samples[
            :, tap_index : tap_index + FRAME_COUNT
        ].astype(jnp.float32)
    filtered = running_sum.astype(jnp.bfloat16)
    fwd = forward_table(FORWARD_LENGTH, CH_LO, channel_total)
    channel_keep_mask = (1 - flagged).astype(jnp.float32)
    frame_spectra = jnp.einsum("afn,kn->akf", filtered, fwd, preferred_element_type=jnp.float32)
    frame_spectra = (
        frame_spectra * FORWARD_LENGTH ** (-0.5) * channel_keep_mask[:, None, None]
    ).astype(jnp.bfloat16)
    frame_spectra = frame_spectra.reshape(antenna_slice, 2, channel_total, FRAME_COUNT)

    def product(pair, right):
        leading, residue = pair
        first = jnp.einsum("cft,ctb->fbc", leading, right, preferred_element_type=jnp.float32)
        return first + jnp.einsum(
            "cft,ctb->fbc", residue, right, preferred_element_type=jnp.float32
        )

    all_index = lax.all_gather(antenna_weight_index, "gx", axis=0, tiled=True)
    onehot_rows = make_onehot(all_index)
    sums = jnp.einsum(
        "arcf,at->rcft",
        lax.all_to_all(frame_spectra, "gx", split_axis=2, concat_axis=0, tiled=True),
        onehot_rows,
        preferred_element_type=jnp.float32,
    )
    leading = sums.astype(jnp.bfloat16)
    residue = (sums - leading.astype(jnp.float32)).astype(jnp.bfloat16)
    real_pair = (leading[0], residue[0])
    imag_pair = (leading[1], residue[1])
    real_part = product(real_pair, weights[0]) - product(imag_pair, weights[1])
    imag_part = product(real_pair, weights[1]) + product(imag_pair, weights[0])
    beams = jnp.stack([real_part, imag_part]).astype(jnp.bfloat16)
    turned = lax.all_to_all(beams, "gx", split_axis=2, concat_axis=3, tiled=True)
    chirped = chirp_apply(turned, trials, channel_total)
    inv = inverse_table(channel_total)
    result = jnp.einsum("rfbc,rcsd->sfbd", chirped, inv, preferred_element_type=jnp.float32)
    return result * channel_total ** (-0.5)


def solution(mesh):
    return jax.shard_map(
        per_device,
        mesh=mesh,
        in_specs=(
            P(("grp", "gx"), None),
            P(),
            P(None, "gx", None, None),
            P(("grp", "gx")),
            P(("grp", "gx")),
            P(("grp", "gx")),
        ),
        out_specs=P(None, None, ("grp", "gx"), None),
        check_vma=False,
    )
```

profile of v0, /device:TPU:0, one launch (start us, length us, event | category | flops | bytes accessed | tf_op | source)
XLA Modules:
  0.0 76.3 jit_solution(12419219289880848327)
XLA Ops:
  0.0 0.0 copy-start.1
  0.0 1.1 %fusion.58 = (f32[1,4096]{1,0:T(1,128)S(1)}, f32[1,4096]{1,0:T(1,128)S(1)}, f32[1,4096]{1,0:T(1,128)S(1)}, f32[1,4096]{1,0:T(1,128)S(1)}) fusion(f32[4,4096]{1,0:T(4,128)} %param.7), kind=kLoop, calls=%fused_computation.96 | loop fusion | bytes 131072 | tf_op jit(solution)/shard_map/slice | solution.py:68
  1.1 4.9 %cosine_convert_fusion = (bf16[64,4096]{1,0:T(8,128)(2,1)S(1)}, bf16[64,4096]{1,0:T(8,128)(2,1)S(1)}) fusion(s32[64]{0:T(128)S(1)} %iota_add_fusion), kind=kLoop, calls=%fused_computation.28 | loop fusion | flops 4456448 | bytes 1048832 | tf_op jit(solution)/shard_map/convert.10
  6.0 10.3 %reshape.203 = bf16[32,35,4096]{2,1,0:T(8,128)(2,1)} reshape(bf16[32,143360]{1,0:T(8,128)(2,1)} %param.6) | data formatting | bytes 18350080 | tf_op jit(solution)/shard_map/reshape | solution.py:65
  16.3 0.0 copy-done.1
  16.3 0.0 copy-start.4
  16.3 0.0 copy-start.2
  16.3 0.0 copy-start.3
  16.4 0.0 copy-start
  16.4 17.2 %fusion.5 = bf16[32,128,32]{1,2,0:T(8,128)(2,1)S(1)} fusion(bf16[32,35,4096]{2,1,0:T(8,128)(2,1)} %reshape.203, f32[4096]{0:T(1024)S(1)} %bitcast.112, f32[4096]{0:T(1024)S(1)} %bitcast.113, f32[4096]{0:T(1024)S(1)} %bitcast.111, f32[4096]{0:T(1024)S(1)} %bitcast.110, bf16[64,4096]{1,0:T(8,128)(2,1)S(1)} %get-tuple-element.20, ...), kind=kOutput, calls=%fused_computation.10 | convolution fusion | flops 1126432768 | bytes 34930816 | tf_op jit(solution)/shard_map/afn,kn->akf/dot_general | solution.py:74
  33.5 0.2 reshape.204
  33.8 1.7 %copy.24 = bf16[32,2,64,32]{3,0,1,2:T(8,128)(2,1)S(1)} copy(bf16[32,2,64,32]{2,1,3,0:T(2,128)(2,1)S(1)} %reshape.204) | data formatting | bytes 524288 | tf_op jit(solution)/shard_map/reshape | solution.py:78
  35.4 1.7 %reshape.217 = bf16[16,2,4096]{2,1,0:T(2,128)(2,1)} reshape(bf16[64,2,32,32]{3,2,1,0:T(8,128)(2,1)S(1)} %bitcast.103) | data formatting | bytes 524288
  37.1 7.4 %all-to-all-start = ((bf16[16,2,4096]{2,1,0:T(2,128)(2,1)}), bf16[16,2,4096]{2,1,0:T(2,128)(2,1)S(1)}, u32[]{:S(2)}, u32[]{:S(2)}) async-start(bf16[16,2,4096]{2,1,0:T(2,128)(2,1)} %reshape.217), calls=%async_computation | async-start | bytes 524288 | tf_op jit(solution)/shard_map/all_to_all | solution.py:91
  44.6 0.2 negate_convert_fusion.1
  44.7 0.0 copy-done.4
  44.7 0.6 dynamic-slice
  46.0 0.0 copy-done.2
  46.0 0.2 dynamic-update-slice
  46.3 12.4 %all-reduce = s32[512]{0:T(512)S(1)} all-reduce(s32[512]{0:T(512)S(1)} %dynamic-update-slice), channel_id=1, replica_groups=mesh['grp'=2,'gx'=16] {'gx'}, use_global_device_ids=true, to_apply=%add | all-reduce | flops 512 | bytes 4096
  58.7 0.0 copy-done.3
  58.7 0.1 multiply_cosine_fusion
  58.8 0.0 all-to-all-done
  58.8 0.5 reshape.218
  59.3 1.0 %copy.26 = bf16[16,32,2,4,32]{1,0,4,3,2:T(8,128)(2,1)S(1)} copy(bf16[16,32,2,4,32]{4,1,2,3,0:T(8,128)(2,1)S(1)} %bitcast.104) | data formatting | bytes 524288 | tf_op jit(solution)/shard_map/all_to_all | solution.py:91
  60.3 1.0 %all_to_all.27 = bf16[512,2,4,32]{0,3,2,1:T(8,128)(2,1)S(1)} reshape(bf16[16,32,2,4,32]{1,0,4,3,2:T(8,128)(2,1)S(1)} %copy.26) | data formatting | bytes 524288 | tf_op jit(solution)/shard_map/all_to_all | solution.py:91
  61.3 0.3 subtract_convert_fusion
  61.6 0.0 copy-done
  61.6 0.2 fusion.33
  61.8 0.2 fusion.27
  62.0 0.2 fusion.24
  62.1 0.2 fusion.30
  62.3 0.2 convolution_add_fusion.3
  62.5 0.2 convolution_add_fusion.1
  62.7 0.2 fusion.11
  62.8 0.2 fusion.10
  63.0 0.2 copy.27
  63.2 0.9 %reshape.219 = bf16[16,2,1024]{2,1,0:T(2,128)(2,1)} reshape(bf16[128,2,4,32]{3,2,1,0:T(4,128)(2,1)S(1)} %bitcast.106) | data formatting | bytes 131072
  64.1 3.5 %all-to-all-start.1 = ((bf16[16,2,1024]{2,1,0:T(2,128)(2,1)}), bf16[16,2,1024]{2,1,0:T(2,128)(2,1)S(1)}, u32[]{:S(2)}, u32[]{:S(2)}) async-start(bf16[16,2,1024]{2,1,0:T(2,128)(2,1)} %reshape.219), calls=%async_computation.1 | async-start | bytes 131072 | tf_op jit(solution)/shard_map/all_to_all | solution.py:102
  67.7 0.1 fusion.55
  67.8 6.7 %all-to-all-done.1 = bf16[16,2,1024]{2,1,0:T(2,128)(2,1)S(1)} async-done(((bf16[16,2,1024]{2,1,0:T(2,128)(2,1)}), bf16[16,2,1024]{2,1,0:T(2,128)(2,1)S(1)}, u32[]{:S(2)}, u32[]{:S(2)}) %all-to-all-start.1) | async-done | bytes 65568 | tf_op jit(solution)/shard_map/all_to_all | solution.py:102
  74.5 0.2 reshape.220
  74.8 0.1 copy.30
  75.0 0.1 copy.32
  75.1 0.1 subtract_convert_fusion.1
  75.2 0.2 fusion.4
  75.4 0.9 %copy.35 = f32[2,32,8,64]{3,2,1,0:T(8,128)} copy(f32[2,32,8,64]{3,1,2,0:T(8,128)S(1)} %fusion.4) | data formatting | bytes 262144 | tf_op jit(solution)/shard_map/mul | solution.py:106
  (11 shorter events, 0.2 us)
Async XLA Ops:
  0.0 16.3 %copy-start.1 = (s32[32]{0:T(128)S(1)}, s32[32]{0:T(128)}, u32[]{:S(2)}) copy-start(s32[32]{0:T(128)} %param.10) | copy-start | bytes 388
  16.3 28.4 %copy-start.4 = (u32[32]{0:T(128)S(1)}, u32[32]{0:T(128)}, u32[]{:S(2)}) copy-start(u32[32]{0:T(128)} %constant.51) | copy-start | bytes 388
  16.3 29.7 %copy-start.2 = (s32[32]{0:T(128)S(1)}, s32[32]{0:T(128)}, u32[]{:S(2)}) copy-start(s32[32]{0:T(128)} %param.9) | copy-start | bytes 388
  16.3 42.3 %copy-start.3 = (s32[8]{0:T(128)S(1)}, s32[8]{0:T(128)}, u32[]{:S(2)}) copy-start(s32[8]{0:T(128)} %param.11) | copy-start | bytes 100
  16.4 45.3 %copy-start = (bf16[2,4,256,128]{3,2,1,0:T(8,128)(2,1)S(1)}, bf16[2,4,256,128]{3,2,1,0:T(8,128)(2,1)}, u32[]{:S(2)}) copy-start(bf16[2,4,256,128]{3,2,1,0:T(8,128)(2,1)} %param.8) | copy-start | bytes 1572868
  37.1 21.6 %all-to-all-start = ((bf16[16,2,4096]{2,1,0:T(2,128)(2,1)}), bf16[16,2,4096]{2,1,0:T(2,128)(2,1)S(1)}, u32[]{:S(2)}, u32[]{:S(2)}) async-start(bf16[16,2,4096]{2,1,0:T(2,128)(2,1)} %reshape.217), calls=%async_computation | async-start | bytes 524288 | tf_op jit(solution)/shard_map/all_to_all | solution.py:91
  64.1 10.4 %all-to-all-start.1 = ((bf16[16,2,1024]{2,1,0:T(2,128)(2,1)}), bf16[16,2,1024]{2,1,0:T(2,128)(2,1)S(1)}, u32[]{:S(2)}, u32[]{:S(2)}) async-start(bf16[16,2,1024]{2,1,0:T(2,128)(2,1)} %reshape.219), calls=%async_computation.1 | async-start | bytes 131072 | tf_op jit(solution)/shard_map/all_to_all | solution.py:102
where the time goes:
time: 76.7 us; the launch traced here: 76.3 us
  local copies, waits for them, and re-layouts  20.8 us (27%)
  matrix products  19 us (25%)
  blocking collectives  12.4 us (16%)
  starting transfers between devices  10.9 us (14%)
  waiting for transfers between devices  6.69 us (9%)
  other arithmetic  5.45 us (7%)
  between operations  0.95 us (1%)
    dot_general x1, matrix products, per_device(): jnp.einsum('afn,kn->akf', filtered, fwd, preferred_element_type=jnp.float32)  17.2 us
    unnamed x1, blocking collectives  12.4 us
    reshape x1, local copies, waits for them, and re-layouts, per_device(): voltages.reshape(antenna_slice, FRAME_COUNT + TAP_COUNT - 1, FORWARD_LENGTH)  10.3 us
    all_to_all x1, starting transfers between devices, per_device(): lax.all_to_all(frame_spectra, 'gx', split_axis=2, concat_axis=0, tiled=True)  7.41 us
    all_to_all x1, waiting for transfers between devices, per_device(): lax.all_to_all(beams, 'gx', split_axis=2, concat_axis=3, tiled=True)  6.69 us
    another operation x4, other arithmetic  5.26 us
    unnamed x17, local copies, waits for them, and re-layouts  4.18 us
    all_to_all x1, starting transfers between devices, per_device(): lax.all_to_all(beams, 'gx', split_axis=2, concat_axis=3, tiled=True)  3.5 us
  transfers between devices with their start and end apart: 2, of which 1 were waited for; matrix products, arithmetic and copies ran while one was open for 2% of the time, Pallas kernels for 0%

commit v1 on v0

v1 whole, which is shorter than its diff:
```python
import functools
import math

import jax
import jax.numpy as jnp
import numpy as np
from jax import lax
from jax.experimental import pallas as pl
from jax.experimental.pallas import tpu as pltpu
from jax.sharding import PartitionSpec as P

FRAME_COUNT = 32
FORWARD_LENGTH = 4096
TAP_COUNT = 4
CH_LO = 1024
WEIGHT_ROWS = 256
LANES = 128
DM_UNIT = 0.173
MESH = pl.DeviceIdType.MESH
NT = (((1,), (1,)), ((), ()))


def twiddles(channels, owners):
    local = channels // owners
    kept = (np.arange(owners)[:, None, None] * local + np.arange(local)[None, None, :]) + np.zeros((1, 2, 1), np.int64)
    part = np.zeros((owners, 1, local), np.int64) + np.arange(2)[None, :, None]
    kept, part = kept.reshape(-1, 1), part.reshape(-1, 1)
    coarse = (CH_LO + kept) * (np.arange(FORWARD_LENGTH // LANES) * LANES)[None] % FORWARD_LENGTH
    fine = (CH_LO + kept) * np.arange(LANES)[None] % FORWARD_LENGTH
    unit = 2.0 * math.pi / FORWARD_LENGTH
    ch, sh = np.cos(coarse * unit), np.sin(coarse * unit)
    first = np.where(part == 0, ch, -sh)
    second = np.where(part == 0, -sh, -ch)
    pad = np.zeros((first.shape[0], LANES - 2 * first.shape[1]))
    return (
        np.concatenate([first, second, pad], 1).astype(np.float32),
        np.stack([np.cos(fine * unit), np.sin(fine * unit)]).astype(np.float32),
    )


def inverse_rows(channels, owners):
    local = channels // owners
    chan = (np.arange(owners)[None, :] * local + np.arange(local)[:, None])[:, None, :, None]
    time = np.arange(channels)[None, None, None, :]
    angle = (chan * time % channels) * (2.0 * math.pi / channels)
    cosine, sine = np.cos(angle), np.sin(angle)
    real = np.concatenate([cosine, -sine], 1)
    imag = np.concatenate([sine, cosine], 1)
    return np.concatenate([real, imag], 3).reshape(2 * channels, 2 * channels).astype(jnp.bfloat16)


def spectra_kernel(group, steps, volts, taps, coarse, fine, keep, out, table, tapped):
    step = pl.program_id(0)
    rows = coarse.shape[0]
    antennas = volts.shape[0]
    frames = FRAME_COUNT

    @pl.when(step == 0)
    def _():
        half = FORWARD_LENGTH // LANES
        for tile in range(half):
            span = slice(tile * LANES, (tile + 1) * LANES)
            base = (
                coarse[:, tile : tile + 1] * fine[0]
                + coarse[:, half + tile : half + tile + 1] * fine[1]
            )
            for tap in range(TAP_COUNT):
                table[tap * rows : (tap + 1) * rows, span] = (base * taps[tap : tap + 1, span]).astype(jnp.bfloat16)

    left = jnp.concatenate(
        [volts[:, g * FORWARD_LENGTH : (g + 1) * FORWARD_LENGTH] for g in range(group)], 0
    )
    block = group * antennas
    tapped[pl.ds(pl.multiple_of(step * block, block), block), :] = lax.dot_general(
        left, table[...], NT, preferred_element_type=jnp.float32
    )

    per_tile = LANES // antennas

    def emit(tile):
        for part in range(rows // LANES):
            pieces = []
            for f in range(tile * per_tile, (tile + 1) * per_tile):
                total = None
                for tap in range(TAP_COUNT):
                    term = tapped[
                        (f + tap) * antennas : (f + tap + 1) * antennas,
                        tap * rows + part * LANES : tap * rows + (part + 1) * LANES,
                    ]
                    total = term if total is None else total + term
                pieces.append(total * keep[...])
            turned = jnp.concatenate(pieces, 0).T
            eights = LANES // out.shape[1]
            out[part * eights : (part + 1) * eights, :, tile * LANES : (tile + 1) * LANES] = turned.reshape(
                eights, out.shape[1], LANES
            ).astype(jnp.bfloat16)

    ready = 0
    for at in range(steps):
        done = min(((at + 1) * group - TAP_COUNT + 1) // per_tile, frames // per_tile)
        tiles = range(ready, done)
        ready = done

        @pl.when(step == at)
        def _(tiles=tiles):
            for tile in tiles:
                emit(tile)


def spectra(voltages, taps, flagged, channels, owners):
    antennas = voltages.shape[0]
    total = FRAME_COUNT + TAP_COUNT - 1
    group = 7
    steps = total // group
    rows = 2 * channels
    coarse, fine = twiddles(channels, owners)
    keep = jnp.broadcast_to(
        ((1 - flagged).astype(jnp.float32) * FORWARD_LENGTH ** (-0.5))[:, None], (antennas, LANES)
    )
    local = rows // owners
    whole = lambda shape: pl.BlockSpec(shape, lambda i: (0,) * len(shape))
    return pl.pallas_call(
        functools.partial(spectra_kernel, group, steps),
        grid=(steps,),
        out_shape=jax.ShapeDtypeStruct((owners, local, FRAME_COUNT * antennas), jnp.bfloat16),
        in_specs=[
            pl.BlockSpec((antennas, group * FORWARD_LENGTH), lambda i: (0, i)),
            whole(taps.shape),
            whole(coarse.shape),
            whole(fine.shape),
            whole(keep.shape),
        ],
        out_specs=whole((owners, local, FRAME_COUNT * antennas)),
        scratch_shapes=[
            pltpu.VMEM((TAP_COUNT * rows, FORWARD_LENGTH), jnp.bfloat16),
            pltpu.VMEM((total * antennas, TAP_COUNT * rows), jnp.float32),
        ],
        compiler_params=pltpu.CompilerParams(dimension_semantics=("arbitrary",)),
        name="spectra",
    )(voltages, taps, jnp.asarray(coarse), jnp.asarray(fine), keep)


def beams_kernel(
    n, spec, index, weights, chirp, inverse, out,
    got_index, got_spec, gathered, lined, sending, got_beams, turned,
    send_sems, index_sems, spec_sems, beam_sems,
):
    me = lax.axis_index("gx")
    locals_ = weights.shape[1]
    beam_total = weights.shape[3]
    frames = FRAME_COUNT
    antennas = spec.shape[2] // frames
    quad = LANES // antennas
    parts = 2 * locals_
    beams = sending.shape[1] // 2

    barrier = pltpu.get_barrier_semaphore()
    for d in range(1, n):
        pl.semaphore_signal(barrier, inc=1, device_id={"gx": lax.rem(me + d, n)}, device_id_type=MESH)
    pl.semaphore_wait(barrier, n - 1)

    def copies(which, source, target, sems, per_peer):
        made = []
        for d in range(1, n):
            peer = lax.rem(me + d, n)
            made.append(
                pltpu.make_async_remote_copy(
                    src_ref=source.at[peer] if per_peer else source,
                    dst_ref=target.at[me],
                    send_sem=send_sems.at[which, d],
                    recv_sem=sems.at[d],
                    device_id={"gx": peer},
                    device_id_type=MESH,
                )
            )
        for copy in made:
            copy.start()
        return made

    def arrivals(which, source, target, sems, per_peer):
        for d in range(1, n):
            peer = lax.rem(me + n - d, n)
            pltpu.make_async_remote_copy(
                src_ref=source.at[peer] if per_peer else source,
                dst_ref=target.at[peer],
                send_sem=send_sems.at[which, d],
                recv_sem=sems.at[d],
                device_id={"gx": peer},
                device_id_type=MESH,
            ).wait_recv()

    first = copies(0, index, got_index, index_sems, False)
    second = copies(1, spec, got_spec, spec_sems, True)
    got_index[me] = index[...]
    got_spec[me] = spec[me]

    arrivals(0, index, got_index, index_sems, False)
    lane = lax.broadcasted_iota(jnp.int32, (LANES, LANES), 1)
    lane_row = lax.broadcasted_iota(jnp.int32, (8, LANES), 1)
    for ag in range(n // quad):
        row = got_index[ag * quad]
        for q in range(1, quad):
            row = jnp.where(lane_row // antennas == q, got_index[ag * quad + q], row)
        column = jnp.broadcast_to(row[0:1].astype(jnp.float32), (LANES, LANES)).T
        column = column.astype(jnp.int32)
        onehot = jnp.concatenate(
            [
                jnp.where(column == lane + t * LANES, 1.0, 0.0).astype(jnp.bfloat16)
                for t in range(WEIGHT_ROWS // LANES)
            ],
            1,
        )
        for c in range(locals_):
            for r in range(2):
                gathered[c, ag * LANES : (ag + 1) * LANES, r * beam_total : (r + 1) * beam_total] = jnp.dot(
                    onehot, weights[r, c], preferred_element_type=jnp.float32
                ).astype(jnp.bfloat16)

    arrivals(1, spec, got_spec, spec_sems, True)
    lane_part = lax.broadcasted_iota(jnp.int32, (parts, LANES), 1) // antennas
    for sg in range(n // quad):
        for ft in range(frames // quad):
            pieces = [
                got_spec[sg * quad + s, :, ft * LANES : (ft + 1) * LANES].astype(jnp.float32)
                for s in range(quad)
            ]
            for f in range(quad):
                made = None
                for s in range(quad):
                    piece = pieces[s]
                    if s != f:
                        piece = pltpu.roll(piece, ((s - f) * antennas) % LANES, 1)
                    made = piece if made is None else jnp.where(lane_part == s, piece, made)
                at = (ft * quad + f) * parts
                lined[sg, at : at + parts, :] = made

    real, imag = [], []
    for c in range(locals_):
        left = jnp.concatenate(
            [
                jnp.concatenate(
                    [lined[sg, pl.ds(r * locals_ + c, frames, stride=parts), :] for sg in range(n // quad)], 1
                )
                for r in range(2)
            ],
            0,
        ).astype(jnp.bfloat16)
        both = jnp.dot(left, gathered[c], preferred_element_type=jnp.float32)
        real.append(both[:frames, :beam_total] - both[frames:, beam_total:])
        imag.append(both[:frames, beam_total:] + both[frames:, :beam_total])
    real, imag = jnp.concatenate(real, 0), jnp.concatenate(imag, 0)
    owners = LANES // beams
    for bt in range(beam_total // LANES):
        span = slice(bt * LANES, (bt + 1) * LANES)
        pair = [x[:, span].T.reshape(owners, beams, LANES) for x in (real, imag)]
        sending[bt * owners : (bt + 1) * owners] = jnp.concatenate(pair, 1).astype(jnp.bfloat16)

    third = copies(2, sending, got_beams, beam_sems, True)
    got_beams[me] = sending[me]
    arrivals(2, sending, got_beams, beam_sems, True)

    for s in range(n):
        block = got_beams[s].astype(jnp.float32)
        x, y = block[:beams], block[beams:]
        cosine, sine = chirp[0, s], chirp[1, s]
        turned[pl.ds(s, beams, stride=2 * n), :] = x * cosine - y * sine
        turned[pl.ds(n + s, beams, stride=2 * n), :] = x * sine + y * cosine

    wide = 2 * n
    lines = []
    if wide >= LANES:
        for b in range(beams):
            across = [turned[b * wide + t * LANES : b * wide + (t + 1) * LANES, :].T for t in range(wide // LANES)]
            lines.append(
                jnp.concatenate(
                    [across[t][c * frames : (c + 1) * frames] for c in range(locals_) for t in range(len(across))], 1
                )
            )
    else:
        each = LANES // wide
        place = lax.broadcasted_iota(jnp.int32, (frames, LANES), 1) // wide
        for g in range(beams // each):
            across = turned[g * LANES : (g + 1) * LANES, :].T
            for b in range(each):
                made = None
                for c in range(locals_):
                    piece = across[c * frames : (c + 1) * frames]
                    if b != c:
                        piece = pltpu.roll(piece, ((c - b) * wide) % LANES, 1)
                    made = piece if made is None else jnp.where(place == c, piece, made)
                lines.append(made)
    left = jnp.concatenate(lines, 0).astype(jnp.bfloat16)
    channels = n * locals_
    out[...] = jnp.dot(left, inverse[...], preferred_element_type=jnp.float32) * channels ** (-0.5)

    for copy in first + second + third:
        copy.wait_send()


def per_device(voltages, taps, weights, antenna_weight_index, flagged, trials):
    n = lax.axis_size("gx")
    locals_ = weights.shape[1]
    beam_total = weights.shape[3]
    channels = locals_ * n
    antennas = voltages.shape[0]
    beams = trials.shape[0]
    spec = spectra(voltages, taps, flagged, channels, n)
    index = jnp.broadcast_to(jnp.tile(antenna_weight_index, LANES // antennas)[None], (8, LANES))
    chan = jnp.repeat(jnp.arange(channels, dtype=jnp.int32).reshape(n, locals_), FRAME_COUNT, axis=1)
    chan = chan.astype(jnp.float32) / channels
    phase = (-2.0 * math.pi * DM_UNIT) * (trials.astype(jnp.float32) + 1.0)[None, :, None] * (chan * chan)[:, None, :]
    chirp = jnp.stack([jnp.cos(phase), jnp.sin(phase)])
    inverse = jnp.asarray(inverse_rows(channels, n))
    parts = 2 * locals_
    vmem = pl.BlockSpec(memory_space=pltpu.VMEM)
    result = pl.pallas_call(
        functools.partial(beams_kernel, n),
        out_shape=jax.ShapeDtypeStruct((beams * FRAME_COUNT, 2 * channels), jnp.float32),
        in_specs=[vmem] * 5,
        out_specs=vmem,
        scratch_shapes=[
            pltpu.VMEM((n, 8, LANES), jnp.int32),
            pltpu.VMEM((n, parts, FRAME_COUNT * antennas), jnp.bfloat16),
            pltpu.VMEM((locals_, n * antennas, 2 * beam_total), jnp.bfloat16),
            pltpu.VMEM((n * antennas // LANES, FRAME_COUNT * parts, LANES), jnp.float32),
            pltpu.VMEM((n, 2 * beams, LANES), jnp.bfloat16),
            pltpu.VMEM((n, 2 * beams, LANES), jnp.bfloat16),
            pltpu.VMEM((beams * 2 * n, LANES), jnp.float32),
            pltpu.SemaphoreType.DMA((3, n)),
            pltpu.SemaphoreType.DMA((n,)),
            pltpu.SemaphoreType.DMA((n,)),
            pltpu.SemaphoreType.DMA((n,)),
        ],
        compiler_params=pltpu.CompilerParams(collective_id=0, has_side_effects=True),
        name="beams",
    )(spec, index, weights, chirp, inverse)
    result = result.reshape(beams, FRAME_COUNT, 2, channels)
    return jnp.transpose(result, (2, 1, 0, 3))


def solution(mesh):
    return jax.shard_map(
        per_device,
        mesh=mesh,
        in_specs=(
            P(("grp", "gx"), None),
            P(),
            P(None, "gx", None, None),
            P(("grp", "gx")),
            P(("grp", "gx")),
            P(("grp", "gx")),
        ),
        out_specs=P(None, None, ("grp", "gx"), None),
        check_vma=False,
    )
```

time: 76.7 us -> 41.1 us (0.54)
  Pallas kernels: 0 us -> 34.4 us
  matrix products: 19 us -> 0 us
  local copies, waits for them, and re-layouts: 20.8 us -> 4.11 us
  blocking collectives: 12.4 us -> 0 us
  starting transfers between devices: 10.9 us -> 0 us
  waiting for transfers between devices: 6.69 us -> 0 us
  other arithmetic: 5.45 us -> 2.31 us
  between operations: 0.95 us -> 0.03 us
    pallas_call x0 -> x2, Pallas kernels: none -> 34.4 us  [the longest x1 23.1 us: per_device(): pl.pallas_call(functools.partial(beams_kernel, n), out_shape=jax.ShapeDty...]
    dot_general x11 -> x0, matrix products: 19 us -> none  [the longest x1 17.2 us: per_device(): jnp.einsum('afn,kn->akf', filtered, fwd, preferred_element_type=jnp.float32)]
    unnamed x1 -> x0, blocking collectives: 12.4 us -> none
    all_to_all x2 -> x0, starting transfers between devices: 10.9 us -> none  [the longest x1 7.41 us: per_device(): lax.all_to_all(frame_spectra, 'gx', split_axis=2, concat_axis=0, tiled=True)]
    reshape x3 -> x2, local copies, waits for them, and re-layouts: 12.2 us -> 1.95 us  [per_device(): result = result.reshape(beams, FRAME_COUNT, 2, channels)]
    all_to_all x2 -> x0, waiting for transfers between devices: 6.69 us -> none  [the longest x1 6.69 us: per_device(): lax.all_to_all(beams, 'gx', split_axis=2, concat_axis=3, tiled=True)]
    another operation x6 -> x1, other arithmetic: 5.29 us -> 0.66 us  [per_device(): chirp = jnp.stack([jnp.cos(phase), jnp.sin(phase)])]
    unnamed x17 -> x0, local copies, waits for them, and re-layouts: 4.18 us -> none
  transfers between devices with their start and end apart: 2 -> 0, of which waited for: 1 -> 0; matrix products, arithmetic and copies ran while one was open for 2% -> 0% of each run, Pallas kernels for 0% -> 0%
where the time goes in v1:
time: 41.1 us; the launch traced here: 40.9 us
  Pallas kernels  34.4 us (84%)
  local copies, waits for them, and re-layouts  4.11 us (10%)
  other arithmetic  2.31 us (6%)
    pallas_call x1, Pallas kernels, per_device(): pl.pallas_call(functools.partial(beams_kernel, n), out_shape=jax.ShapeDty...  23.1 us
    pallas_call x1, Pallas kernels, spectra(): pl.pallas_call(functools.partial(spectra_kernel, group, steps), grid=(ste...  11.3 us
    reshape x2, local copies, waits for them, and re-layouts, per_device(): result = result.reshape(beams, FRAME_COUNT, 2, channels)  1.95 us

profile of v1, /device:TPU:0, one launch (start us, length us, event | category | flops | bytes accessed | tf_op | source)
XLA Modules:
  0.0 40.9 jit_solution(18254003131312903701)
XLA Ops:
  0.0 0.7 %convert_multiply_fusion = f32[32]{0:T(128)S(1)} fusion(s32[32]{0:T(128)} %param.13), kind=kLoop, calls=%fused_computation.6 | loop fusion | flops 96 | bytes 256 | tf_op jit(solution)/shard_map/mul | solution.py:118
  0.7 0.7 %add_multiply_fusion = f32[8]{0:T(128)S(1)} fusion(s32[8]{0:T(128)} %param.14), kind=kLoop, calls=%fused_computation.5 | loop fusion | flops 24 | bytes 64 | tf_op jit(solution)/shard_map/mul | solution.py:311
  1.3 0.7 %tile.2 = s32[4,32]{1,0:T(4,128)S(1)} broadcast(s32[32]{0:T(128)} %param.12), dimensions={1} | broadcast | bytes 640 | tf_op jit(solution)/shard_map/tile | solution.py:308
  2.0 0.1 broadcast_in_dim.9
  2.1 0.6 %broadcast_in_dim.20.index = s32[8,128]{1,0:T(8,128)} broadcast(s32[128]{0:T(128)S(1)} %broadcast_in_dim.9), dimensions={1} | broadcast | bytes 4608 | tf_op jit(solution)/shard_map/broadcast_in_dim | solution.py:308
  2.7 0.7 %broadcast_in_dim.8.keep = f32[32,128]{1,0:T(8,128)} broadcast(f32[32]{0:T(128)S(1)} %convert_multiply_fusion), dimensions={0} | broadcast | bytes 16512 | tf_op jit(solution)/shard_map/broadcast_in_dim | solution.py:117
  3.3 0.1 broadcast_in_dim.21
  3.4 0.1 mul.50
  3.5 0.3 multiply_cosine_fusion
  3.8 0.7 %pad_maximum_fusion.chirp = f32[2,16,8,128]{3,2,1,0:T(8,128)} fusion(f32[1,16,8,128]{3,2,1,0:T(8,128)S(1)} %get-tuple-element.6, f32[1,16,8,128]{3,2,1,0:T(8,128)S(1)} %get-tuple-element.5), kind=kLoop, calls=%fused_computation.1 | loop fusion | flops 32768 | bytes 262144 | tf_op jit(solution)/shard_map/stack | solution.py:312
  4.5 11.3 %spectra.1.spec = bf16[16,8,1024]{2,1,0:T(8,128)(2,1)} custom-call(bf16[32,143360]{1,0:T(8,128)(2,1)} %volts.1, f32[4,4096]{1,0:T(4,128)} %taps.1, f32[128,128]{1,0:T(8,128)} %constant.18.clone.coarse, f32[2,128,128]{2,1,0:T(8,128)} %constant.19.clone.fine, f32[32,128]{1,0:T(8,128)} %broadcast_in_dim.8.keep), custom_call_target="tpu_custom_call" | custom-call | tf_op jit(solution)/shard_map/spectra/pallas_call | solution.py:122
  15.7 23.1 %beams.1 = f32[256,128]{1,0:T(8,128)} custom-call(bf16[16,8,1024]{2,1,0:T(8,128)(2,1)} %spectra.1.spec, s32[8,128]{1,0:T(8,128)} %broadcast_in_dim.20.index, bf16[2,4,256,128]{3,2,1,0:T(8,128)(2,1)} %weights.1, f32[2,16,8,128]{3,2,1,0:T(8,128)} %pad_maximum_fusion.chirp, bf16[128,128]{1,0:T(8,128)(2,1)} %constant.20.clone.inverse), custom_call_target="tpu_custom_call" | custom-call | tf_op jit(solution)/shard_map/beams/pallas_call | solution.py:316
  38.9 1.1 %reshape.39 = f32[8,32,2,64]{3,2,1,0:T(2,128)S(1)} reshape(f32[256,128]{1,0:T(8,128)} %beams.1) | data formatting | bytes 262144 | tf_op jit(solution)/shard_map/reshape | solution.py:337
  40.0 0.9 %copy.12 = f32[8,32,2,64]{3,0,1,2:T(8,128)} copy(f32[8,32,2,64]{3,2,1,0:T(2,128)S(1)} %reshape.39) | data formatting | bytes 262144 | tf_op jit(solution)/shard_map/reshape | solution.py:337
  (1 shorter events, 0.0 us)

commit v2 on v1

v2 whole, which is shorter than its diff:
```python
import functools
import math

import jax
import jax.numpy as jnp
import numpy as np
from jax import lax
from jax.experimental import pallas as pl
from jax.experimental.pallas import tpu as pltpu
from jax.sharding import PartitionSpec as P

FRAME_COUNT = 32
FORWARD_LENGTH = 4096
TAP_COUNT = 4
CH_LO = 1024
WEIGHT_ROWS = 256
LANES = 128
DM_UNIT = 0.173
MESH = pl.DeviceIdType.MESH
NT = (((1,), (1,)), ((), ()))


def twiddles(channels, owners):
    local = channels // owners
    kept = (np.arange(owners)[:, None, None] * local + np.arange(local)[None, None, :]) + np.zeros((1, 2, 1), np.int64)
    part = np.zeros((owners, 1, local), np.int64) + np.arange(2)[None, :, None]
    kept, part = kept.reshape(-1, 1), part.reshape(-1, 1)
    coarse = (CH_LO + kept) * (np.arange(FORWARD_LENGTH // LANES) * LANES)[None] % FORWARD_LENGTH
    fine = (CH_LO + kept) * np.arange(LANES)[None] % FORWARD_LENGTH
    unit = 2.0 * math.pi / FORWARD_LENGTH
    ch, sh = np.cos(coarse * unit), np.sin(coarse * unit)
    first = np.where(part == 0, ch, -sh)
    second = np.where(part == 0, -sh, -ch)
    pad = np.zeros((first.shape[0], LANES - 2 * first.shape[1]))
    return (
        np.concatenate([first, second, pad], 1).astype(np.float32),
        np.stack([np.cos(fine * unit), np.sin(fine * unit)]).astype(np.float32),
    )


def inverse_rows(channels, owners):
    local = channels // owners
    chan = (np.arange(owners)[None, :] * local + np.arange(local)[:, None])[:, None, :, None]
    time = np.arange(channels)[None, None, None, :]
    angle = (chan * time % channels) * (2.0 * math.pi / channels)
    cosine, sine = np.cos(angle), np.sin(angle)
    real = np.concatenate([cosine, -sine], 1)
    imag = np.concatenate([sine, cosine], 1)
    return np.stack([real, imag]).reshape(2, 2 * channels, channels).astype(jnp.bfloat16)


GROUP = 7


def kernel(
    n, plan, index, flagged, trials, volts_hbm, taps, coarse, fine, weights_hbm, inverse, out,
    volts, weights, table, tapped, keep, chirp, index_row, spec,
    got_index, got_spec, gathered, lined, sending, got_beams, turned, stacked,
    load_sems, send_sems, index_sems, spec_sems, beam_sems,
):
    me = lax.axis_index("gx")
    rows = coarse.shape[0]
    antennas = volts.shape[0]
    locals_ = weights.shape[1]
    beam_total = weights.shape[3]
    channels = n * locals_
    frames = FRAME_COUNT
    quad = LANES // antennas
    parts = 2 * locals_
    beams = sending.shape[1] // 2
    steps = len(plan)

    loads = []
    for at in range(steps):
        span = pl.ds(at * GROUP * FORWARD_LENGTH, GROUP * FORWARD_LENGTH)
        loads.append(pltpu.make_async_copy(volts_hbm.at[:, span], volts.at[:, span], load_sems.at[at]))
    loads.append(pltpu.make_async_copy(weights_hbm, weights, load_sems.at[steps]))
    for load in loads:
        load.start()

    barrier = pltpu.get_barrier_semaphore()
    for d in range(1, n):
        pl.semaphore_signal(barrier, inc=1, device_id={"gx": lax.rem(me + d, n)}, device_id_type=MESH)

    lane_one = lax.broadcasted_iota(jnp.int32, (1, LANES), 1) % antennas
    row = jnp.zeros((1, LANES), jnp.int32)
    for a in range(antennas):
        row = jnp.where(lane_one == a, index[a], row)
    index_row[...] = row
    antenna = lax.broadcasted_iota(jnp.int32, (antennas, LANES), 0)
    off = jnp.zeros((antennas, LANES), jnp.int32)
    for a in range(antennas):
        off = jnp.where(antenna == a, flagged[a], off)
    keep[...] = (1 - off).astype(jnp.float32) * FORWARD_LENGTH ** (-0.5)

    def copies(which, source, target, sems):
        made = []
        for d in range(1, n):
            peer = lax.rem(me + d, n)
            made.append(
                pltpu.make_async_remote_copy(
                    src_ref=source(peer),
                    dst_ref=target(me),
                    send_sem=send_sems.at[which, d],
                    recv_sem=sems.at[d],
                    device_id={"gx": peer},
                    device_id_type=MESH,
                )
            )
        for copy in made:
            copy.start()
        return made

    def arrivals(which, source, target, sems):
        for d in range(1, n):
            peer = lax.rem(me + n - d, n)
            pltpu.make_async_remote_copy(
                src_ref=source(peer),
                dst_ref=target(peer),
                send_sem=send_sems.at[which, d],
                recv_sem=sems.at[d],
                device_id={"gx": peer},
                device_id_type=MESH,
            ).wait_recv()

    index_args = (steps, lambda p: index_row, lambda p: got_index.at[p], index_sems)
    beam_args = (steps + 1, lambda p: sending.at[p], lambda p: got_beams.at[p], beam_sems)

    def piece_args(at):
        span = pl.ds(plan[at][0] * LANES, (plan[at][1] - plan[at][0]) * LANES)
        return (at, lambda p: spec.at[p, :, span], lambda p: got_spec.at[p, :, span], spec_sems.at[at])

    half = FORWARD_LENGTH // LANES
    for tile in range(half):
        span = slice(tile * LANES, (tile + 1) * LANES)
        base = (
            coarse[:, tile : tile + 1] * fine[0]
            + coarse[:, half + tile : half + tile + 1] * fine[1]
        )
        for tap in range(TAP_COUNT):
            table[tap * rows : (tap + 1) * rows, span] = (base * taps[tap : tap + 1, span]).astype(jnp.bfloat16)

    pl.semaphore_wait(barrier, n - 1)
    started = copies(*index_args)
    got_index[me] = index_row[...]

    def emit(tile):
        for part in range(rows // LANES):
            pieces = []
            for f in range(tile * quad, (tile + 1) * quad):
                total = None
                for tap in range(TAP_COUNT):
                    term = tapped[
                        (f + tap) * antennas : (f + tap + 1) * antennas,
                        tap * rows + part * LANES : tap * rows + (part + 1) * LANES,
                    ]
                    total = term if total is None else total + term
                pieces.append(total * keep[...])
            across = jnp.concatenate(pieces, 0).T
            eights = LANES // parts
            spec[part * eights : (part + 1) * eights, :, tile * LANES : (tile + 1) * LANES] = across.reshape(
                eights, parts, LANES
            ).astype(jnp.bfloat16)

    def gather_weights():
        arrivals(*index_args)
        loads[steps].wait()
        lane = lax.broadcasted_iota(jnp.int32, (LANES, LANES), 1)
        lane_quad = lax.broadcasted_iota(jnp.int32, (1, LANES), 1) // antennas
        for ag in range(n // quad):
            row = got_index[ag * quad]
            for q in range(1, quad):
                row = jnp.where(lane_quad == q, got_index[ag * quad + q], row)
            column = jnp.broadcast_to(row.astype(jnp.float32), (LANES, LANES)).T
            column = column.astype(jnp.int32)
            onehot = jnp.concatenate(
                [
                    jnp.where(column == lane + t * LANES, 1.0, 0.0).astype(jnp.bfloat16)
                    for t in range(WEIGHT_ROWS // LANES)
                ],
                1,
            )
            for c in range(locals_):
                for r in range(2):
                    gathered[
                        c, ag * LANES : (ag + 1) * LANES, r * beam_total : (r + 1) * beam_total
                    ] = jnp.dot(onehot, weights[r, c], preferred_element_type=jnp.float32).astype(jnp.bfloat16)

    def turn():
        beam = lax.broadcasted_iota(jnp.int32, (beams, LANES), 0)
        trial = jnp.zeros((beams, LANES), jnp.int32)
        for b in range(beams):
            trial = jnp.where(beam == b, trials[b], trial)
        scaled = (-2.0 * math.pi * DM_UNIT) * (trial.astype(jnp.float32) + 1.0)
        lane_chan = lax.broadcasted_iota(jnp.int32, (n, beams, LANES), 2) // frames
        owner = lax.broadcasted_iota(jnp.int32, (n, beams, LANES), 0)
        chan = (owner * locals_ + lane_chan).astype(jnp.float32) / channels
        phase = scaled[None] * (chan * chan)
        chirp[0] = jnp.cos(phase)
        chirp[1] = jnp.sin(phase)

    for at in range(steps):
        loads[at].wait()
        left = jnp.concatenate(
            [volts[:, g * FORWARD_LENGTH : (g + 1) * FORWARD_LENGTH] for g in range(at * GROUP, (at + 1) * GROUP)], 0
        )
        block = GROUP * antennas
        tapped[at * block : (at + 1) * block, :] = lax.dot_general(
            left, table[...], NT, preferred_element_type=jnp.float32
        )
        for tile in range(*plan[at]):
            emit(tile)
        started += copies(*piece_args(at))
        if at == steps - 2:
            gather_weights()
        if at == steps - 3:
            turn()
    got_spec[me] = spec[me]

    lane_part = lax.broadcasted_iota(jnp.int32, (parts, LANES), 1) // antennas
    for at in range(steps):
        arrivals(*piece_args(at))
        for sg in range(n // quad):
            for ft in range(*plan[at]):
                pieces = [
                    got_spec[sg * quad + s, :, ft * LANES : (ft + 1) * LANES].astype(jnp.float32)
                    for s in range(quad)
                ]
                for f in range(quad):
                    made = None
                    for s in range(quad):
                        piece = pieces[s]
                        if s != f:
                            piece = pltpu.roll(piece, ((s - f) * antennas) % LANES, 1)
                        made = piece if made is None else jnp.where(lane_part == s, piece, made)
                    to = (ft * quad + f) * parts
                    lined[sg, to : to + parts, :] = made

    real, imag = [], []
    for c in range(locals_):
        left = jnp.concatenate(
            [
                jnp.concatenate(
                    [lined[sg, pl.ds(r * locals_ + c, frames, stride=parts), :] for sg in range(n // quad)], 1
                )
                for r in range(2)
            ],
            0,
        ).astype(jnp.bfloat16)
        both = jnp.dot(left, gathered[c], preferred_element_type=jnp.float32)
        real.append(both[:frames, :beam_total] - both[frames:, beam_total:])
        imag.append(both[:frames, beam_total:] + both[frames:, :beam_total])
    real, imag = jnp.concatenate(real, 0), jnp.concatenate(imag, 0)
    owners = LANES // beams
    for bt in range(beam_total // LANES):
        span = slice(bt * LANES, (bt + 1) * LANES)
        pair = [x[:, span].T.reshape(owners, beams, LANES) for x in (real, imag)]
        sending[bt * owners : (bt + 1) * owners] = jnp.concatenate(pair, 1).astype(jnp.bfloat16)

    started += copies(*beam_args)
    got_beams[me] = sending[me]
    arrivals(*beam_args)

    for s in range(n):
        block = got_beams[s].astype(jnp.float32)
        x, y = block[:beams], block[beams:]
        cosine, sine = chirp[0, s], chirp[1, s]
        turned[pl.ds(s, beams, stride=2 * n), :] = x * cosine - y * sine
        turned[pl.ds(n + s, beams, stride=2 * n), :] = x * sine + y * cosine

    wide = 2 * n
    deep = locals_ * wide // LANES
    if wide >= LANES:
        for b in range(beams):
            for t in range(wide // LANES):
                across = turned[b * wide + t * LANES : b * wide + (t + 1) * LANES, :].T
                for c in range(locals_):
                    stacked[c * (wide // LANES) + t, pl.ds(b, frames, stride=beams), :] = across[
                        c * frames : (c + 1) * frames
                    ]
    else:
        each = LANES // wide
        place = lax.broadcasted_iota(jnp.int32, (frames, LANES), 1) // wide
        for g in range(beams // each):
            across = turned[g * LANES : (g + 1) * LANES, :].T
            for b in range(each):
                for k in range(deep):
                    made = None
                    for slot in range(each):
                        c = k * each + slot
                        piece = across[c * frames : (c + 1) * frames]
                        if b != slot:
                            piece = pltpu.roll(piece, ((slot - b) * wide) % LANES, 1)
                        made = piece if made is None else jnp.where(place == slot, piece, made)
                    stacked[k, pl.ds(g * each + b, frames, stride=beams), :] = made
    left = jnp.concatenate([stacked[k] for k in range(deep)], 1).astype(jnp.bfloat16)
    for s in range(2):
        total = jnp.dot(left, inverse[s], preferred_element_type=jnp.float32) * channels ** (-0.5)
        out[s] = total.reshape(frames, beams, channels)

    for copy in started:
        copy.wait_send()


def per_device(voltages, taps, weights, antenna_weight_index, flagged, trials):
    n = lax.axis_size("gx")
    locals_ = weights.shape[1]
    beam_total = weights.shape[3]
    channels = locals_ * n
    antennas = voltages.shape[0]
    beams = trials.shape[0]
    parts = 2 * locals_
    rows = 2 * channels
    total = FRAME_COUNT + TAP_COUNT - 1
    steps = total // GROUP
    coarse, fine = twiddles(channels, n)
    inverse = inverse_rows(channels, n)
    quad = LANES // antennas
    plan, ready = [], 0
    for at in range(steps):
        done = ((at + 1) * GROUP - TAP_COUNT + 1) // quad
        plan.append((ready, done))
        ready = done
    vmem = pl.BlockSpec(memory_space=pltpu.VMEM)
    smem = pl.BlockSpec(memory_space=pltpu.SMEM)
    hbm = pl.BlockSpec(memory_space=pl.ANY)
    return pl.pallas_call(
        functools.partial(kernel, n, plan),
        out_shape=jax.ShapeDtypeStruct((2, FRAME_COUNT, beams, channels), jnp.float32),
        in_specs=[smem, smem, smem, hbm, vmem, vmem, vmem, hbm, vmem],
        out_specs=vmem,
        scratch_shapes=[
            pltpu.VMEM(voltages.shape, jnp.bfloat16),
            pltpu.VMEM(weights.shape, jnp.bfloat16),
            pltpu.VMEM((TAP_COUNT * rows, FORWARD_LENGTH), jnp.bfloat16),
            pltpu.VMEM((total * antennas, TAP_COUNT * rows), jnp.float32),
            pltpu.VMEM((antennas, LANES), jnp.float32),
            pltpu.VMEM((2, n, beams, LANES), jnp.float32),
            pltpu.VMEM((1, LANES), jnp.int32),
            pltpu.VMEM((n, parts, FRAME_COUNT * antennas), jnp.bfloat16),
            pltpu.VMEM((n, 1, LANES), jnp.int32),
            pltpu.VMEM((n, parts, FRAME_COUNT * antennas), jnp.bfloat16),
            pltpu.VMEM((locals_, n * antennas, 2 * beam_total), jnp.bfloat16),
            pltpu.VMEM((n * antennas // LANES, FRAME_COUNT * parts, LANES), jnp.float32),
            pltpu.VMEM((n, 2 * beams, LANES), jnp.bfloat16),
            pltpu.VMEM((n, 2 * beams, LANES), jnp.bfloat16),
            pltpu.VMEM((beams * 2 * n, LANES), jnp.float32),
            pltpu.VMEM((2 * channels // LANES, FRAME_COUNT * beams, LANES), jnp.float32),
            pltpu.SemaphoreType.DMA((steps + 1,)),
            pltpu.SemaphoreType.DMA((steps + 2, n)),
            pltpu.SemaphoreType.DMA((n,)),
            pltpu.SemaphoreType.DMA((steps, n)),
            pltpu.SemaphoreType.DMA((n,)),
        ],
        compiler_params=pltpu.CompilerParams(collective_id=0, has_side_effects=True),
        name="beamformer",
    )(
        antenna_weight_index, flagged, trials, voltages, taps,
        jnp.asarray(coarse), jnp.asarray(fine), weights, jnp.asarray(inverse),
    )


def solution(mesh):
    return jax.shard_map(
        per_device,
        mesh=mesh,
        in_specs=(
            P(("grp", "gx"), None),
            P(),
            P(None, "gx", None, None),
            P(("grp", "gx")),
            P(("grp", "gx")),
            P(("grp", "gx")),
        ),
        out_specs=P(None, None, ("grp", "gx"), None),
        check_vma=False,
    )
```

time: 41.1 us -> 29.8 us (0.73)
  Pallas kernels: 34.4 us -> 28 us
  local copies, waits for them, and re-layouts: 4.11 us -> 1.67 us
  other arithmetic: 2.31 us -> 0 us
    pallas_call x2 -> x1, Pallas kernels: 34.4 us -> 28 us  [per_device(): pl.pallas_call(functools.partial(kernel, n, plan), out_shape=jax.ShapeDty...]
    reshape x2 -> x0, local copies, waits for them, and re-layouts: 1.95 us -> none  [per_device(): result = result.reshape(beams, FRAME_COUNT, 2, channels)]
    unnamed x0 -> x1, local copies, waits for them, and re-layouts: none -> 1.67 us
    broadcast_in_dim x4 -> x0, local copies, waits for them, and re-layouts: 1.42 us -> none  [the longest x2 0.69 us: per_device(): jnp.broadcast_to(jnp.tile(antenna_weight_index, LANES // antennas)[None],...]
    mul x3 -> x0, other arithmetic: 1.33 us -> none  [the longest x1 0.66 us: spectra(): (1 - flagged).astype(jnp.float32) * FORWARD_LENGTH ** (-0.5)]
    another operation x1 -> x0, other arithmetic: 0.66 us -> none  [per_device(): chirp = jnp.stack([jnp.cos(phase), jnp.sin(phase)])]
    another operation x1 -> x0, local copies, waits for them, and re-layouts: 0.66 us -> none  [per_device(): jnp.tile(antenna_weight_index, LANES // antennas)[None]]
where the time goes in v2:
time: 29.8 us; the launch traced here: 29.6 us
  Pallas kernels  28 us (94%)
  local copies, waits for them, and re-layouts  1.67 us (6%)
    pallas_call x1, Pallas kernels, per_device(): pl.pallas_call(functools.partial(kernel, n, plan), out_shape=jax.ShapeDty...  28 us
    unnamed x1, local copies, waits for them, and re-layouts  1.67 us

profile of v2, /device:TPU:0, one launch (start us, length us, event | category | flops | bytes accessed | tf_op | source)
XLA Modules:
  0.0 29.6 jit_solution(8873574335430191124)
XLA Ops:
  0.0 28.0 %beamformer.1 = f32[2,32,8,64]{3,2,1,0:T(8,128)} custom-call(s32[32]{0:T(128)} %index.1, s32[32]{0:T(128)} %flagged.1, s32[8]{0:T(128)} %trials.1, bf16[32,143360]{1,0:T(8,128)(2,1)} %volts_hbm.1, f32[4,4096]{1,0:T(4,128)} %taps.1, f32[128,128]{1,0:T(8,128)} %constant.6.clone.coarse, f32[2,128,128]{2,1,0:T(8,128)} %constant.7.clone.fine, ...), custom_call_target="tpu_custom_call" | custom-call | tf_op jit(solution)/shard_map/beamformer/pallas_call | solution.py:327
  28.0 1.7 %copy.11 = f32[2,32,8,64]{3,2,1,0:T(8,128)} copy(f32[2,32,8,64]{3,2,1,0:T(8,128)} %beamformer.1) | data formatting | bytes 262144

commit v3 on v2

--- a/solution.py
+++ b/solution.py
@@ -75,7 +75,7 @@
         span = pl.ds(at * GROUP * FORWARD_LENGTH, GROUP * FORWARD_LENGTH)
         loads.append(pltpu.make_async_copy(volts_hbm.at[:, span], volts.at[:, span], load_sems.at[at]))
     loads.append(pltpu.make_async_copy(weights_hbm, weights, load_sems.at[steps]))
-    for load in loads:
+    for load in loads[:2]:
         load.start()
 
     barrier = pltpu.get_barrier_semaphore()
@@ -140,9 +140,7 @@
         for tap in range(TAP_COUNT):
             table[tap * rows : (tap + 1) * rows, span] = (base * taps[tap : tap + 1, span]).astype(jnp.bfloat16)
 
-    pl.semaphore_wait(barrier, n - 1)
-    started = copies(*index_args)
-    got_index[me] = index_row[...]
+    started = []
 
     def emit(tile):
         for part in range(rows // LANES):
@@ -201,6 +199,8 @@
 
     for at in range(steps):
         loads[at].wait()
+        if at + 2 < len(loads):
+            loads[at + 2].start()
         left = jnp.concatenate(
             [volts[:, g * FORWARD_LENGTH : (g + 1) * FORWARD_LENGTH] for g in range(at * GROUP, (at + 1) * GROUP)], 0
         )
@@ -210,6 +210,10 @@
         )
         for tile in range(*plan[at]):
             emit(tile)
+        if at == 0:
+            pl.semaphore_wait(barrier, n - 1)
+            started += copies(*index_args)
+            got_index[me] = index_row[...]
         started += copies(*piece_args(at))
         if at == steps - 2:
             gather_weights()
@@ -323,7 +327,7 @@
         ready = done
     vmem = pl.BlockSpec(memory_space=pltpu.VMEM)
     smem = pl.BlockSpec(memory_space=pltpu.SMEM)
-    hbm = pl.BlockSpec(memory_space=pl.ANY)
+    hbm = pl.BlockSpec(memory_space=pltpu.HBM)
     return pl.pallas_call(
         functools.partial(kernel, n, plan),
         out_shape=jax.ShapeDtypeStruct((2, FRAME_COUNT, beams, channels), jnp.float32),

time: 29.8 us -> 28.3 us (0.950)
  Pallas kernels: 28 us -> 26.5 us
    pallas_call x1, Pallas kernels: 28 us -> 26.5 us  [per_device(): pl.pallas_call(functools.partial(kernel, n, plan), out_shape=jax.ShapeDty...]
where the time goes in v3:
time: 28.3 us; the launch traced here: 28.2 us
  Pallas kernels  26.5 us (94%)
  local copies, waits for them, and re-layouts  1.67 us (6%)
    pallas_call x1, Pallas kernels, per_device(): pl.pallas_call(functools.partial(kernel, n, plan), out_shape=jax.ShapeDty...  26.5 us
    unnamed x1, local copies, waits for them, and re-layouts  1.67 us

profile of v3, /device:TPU:0, one launch (start us, length us, event | category | flops | bytes accessed | tf_op | source)
XLA Modules:
  0.0 28.2 jit_solution(9216360793116920137)
XLA Ops:
  0.0 26.5 %beamformer.1 = f32[2,32,8,64]{3,2,1,0:T(8,128)} custom-call(s32[32]{0:T(128)} %index.1, s32[32]{0:T(128)} %flagged.1, s32[8]{0:T(128)} %trials.1, bf16[32,143360]{1,0:T(8,128)(2,1)} %volts_hbm.1, f32[4,4096]{1,0:T(4,128)} %taps.1, f32[128,128]{1,0:T(8,128)} %constant.6.clone.coarse, f32[2,128,128]{2,1,0:T(8,128)} %constant.7.clone.fine, ...), custom_call_target="tpu_custom_call" | custom-call | tf_op jit(solution)/shard_map/beamformer/pallas_call | solution.py:331
  26.5 1.7 %copy.11 = f32[2,32,8,64]{3,2,1,0:T(8,128)} copy(f32[2,32,8,64]{3,2,1,0:T(8,128)} %beamformer.1) | data formatting | bytes 262144

commit v4 on v3

--- a/solution.py
+++ b/solution.py
@@ -49,7 +49,7 @@
     return np.stack([real, imag]).reshape(2, 2 * channels, channels).astype(jnp.bfloat16)
 
 
-GROUP = 7
+GROUPS = (8, 8, 8, 8, 3)
 
 
 def kernel(
@@ -72,7 +72,7 @@
 
     loads = []
     for at in range(steps):
-        span = pl.ds(at * GROUP * FORWARD_LENGTH, GROUP * FORWARD_LENGTH)
+        span = pl.ds(sum(GROUPS[:at]) * FORWARD_LENGTH, GROUPS[at] * FORWARD_LENGTH)
         loads.append(pltpu.make_async_copy(volts_hbm.at[:, span], volts.at[:, span], load_sems.at[at]))
     loads.append(pltpu.make_async_copy(weights_hbm, weights, load_sems.at[steps]))
     for load in loads[:2]:
@@ -201,11 +201,11 @@
         loads[at].wait()
         if at + 2 < len(loads):
             loads[at + 2].start()
+        begin = sum(GROUPS[:at])
         left = jnp.concatenate(
-            [volts[:, g * FORWARD_LENGTH : (g + 1) * FORWARD_LENGTH] for g in range(at * GROUP, (at + 1) * GROUP)], 0
+            [volts[:, g * FORWARD_LENGTH : (g + 1) * FORWARD_LENGTH] for g in range(begin, begin + GROUPS[at])], 0
         )
-        block = GROUP * antennas
-        tapped[at * block : (at + 1) * block, :] = lax.dot_general(
+        tapped[begin * antennas : (begin + GROUPS[at]) * antennas, :] = lax.dot_general(
             left, table[...], NT, preferred_element_type=jnp.float32
         )
         for tile in range(*plan[at]):
@@ -316,13 +316,13 @@
     parts = 2 * locals_
     rows = 2 * channels
     total = FRAME_COUNT + TAP_COUNT - 1
-    steps = total // GROUP
+    steps = len(GROUPS)
     coarse, fine = twiddles(channels, n)
     inverse = inverse_rows(channels, n)
     quad = LANES // antennas
     plan, ready = [], 0
     for at in range(steps):
-        done = ((at + 1) * GROUP - TAP_COUNT + 1) // quad
+        done = (sum(GROUPS[: at + 1]) - TAP_COUNT + 1) // quad
         plan.append((ready, done))
         ready = done
     vmem = pl.BlockSpec(memory_space=pltpu.VMEM)
@@ -356,7 +356,7 @@
             pltpu.SemaphoreType.DMA((steps, n)),
             pltpu.SemaphoreType.DMA((n,)),
         ],
-        compiler_params=pltpu.CompilerParams(collective_id=0, has_side_effects=True),
+        compiler_params=pltpu.CompilerParams(collective_id=0, has_side_effects=True, vmem_limit_bytes=67043328),
         name="beamformer",
     )(
         antenna_weight_index, flagged, trials, voltages, taps,

time: 28.3 us -> 27.7 us (0.979)
  Pallas kernels: 26.5 us -> 25.9 us
    pallas_call x1, Pallas kernels: 26.5 us -> 25.9 us  [per_device(): pl.pallas_call(functools.partial(kernel, n, plan), out_shape=jax.ShapeDty...]
where the time goes in v4:
time: 27.7 us; the launch traced here: 27.6 us
  Pallas kernels  25.9 us (94%)
  local copies, waits for them, and re-layouts  1.67 us (6%)
    pallas_call x1, Pallas kernels, per_device(): pl.pallas_call(functools.partial(kernel, n, plan), out_shape=jax.ShapeDty...  25.9 us
    unnamed x1, local copies, waits for them, and re-layouts  1.67 us

profile of v4, /device:TPU:0, one launch (start us, length us, event | category | flops | bytes accessed | tf_op | source)
XLA Modules:
  0.0 27.6 jit_solution(2251534225790388976)
XLA Ops:
  0.0 25.9 %beamformer.1 = f32[2,32,8,64]{3,2,1,0:T(8,128)} custom-call(s32[32]{0:T(128)} %index.1, s32[32]{0:T(128)} %flagged.1, s32[8]{0:T(128)} %trials.1, bf16[32,143360]{1,0:T(8,128)(2,1)} %volts_hbm.1, f32[4,4096]{1,0:T(4,128)} %taps.1, f32[128,128]{1,0:T(8,128)} %constant.6.clone.coarse, f32[2,128,128]{2,1,0:T(8,128)} %constant.7.clone.fine, ...), custom_call_target="tpu_custom_call" | custom-call | tf_op jit(solution)/shard_map/beamformer/pallas_call | solution.py:331
  25.9 1.7 %copy.11 = f32[2,32,8,64]{3,2,1,0:T(8,128)} copy(f32[2,32,8,64]{3,2,1,0:T(8,128)} %beamformer.1) | data formatting | bytes 262144
